TPU v7x, 256 devices: a whole 4x4x8 slice. The times are simulated.
256 devices in a mesh: batch: 4 (over y), lat: 8 (over x, core), lon: 8 (over z).
Axes of the slice: x: 4, y: 4, z: 8, core: 2. Of those that a mesh axis runs over, the one named last changes fastest.
Arguments:
- patches: bfloat16 [4, 16, 24, 128, 640], P('batch', 'lat', 'lon'), may hold values from -6 to 6
- kept_index: int32 [4, 16, 24, 64], P('batch', 'lat', 'lon'), may hold values from 0 to 127, as said below
- kept_count: int32 [4, 16, 24], P('batch', 'lat', 'lon'), may hold values from 32 to 64, as said below
- embed_weight: bfloat16 [640, 1280], P('batch'), may hold values from -0.25 to 0.25
- local_qkv: bfloat16 [1280, 3840], P('batch'), may hold values from -6 to 6
- local_out: bfloat16 [1280, 1280], P('batch'), may hold values from -0.15625 to 0.15625
- global_qkv: bfloat16 [1280, 3840], P('batch'), may hold values from -6 to 6
Outputs:
- mixed: bfloat16 [4, 16, 24, 64, 1280], P('batch', 'lat', 'lon')
Inputs may be any that keep to these rules, and one draw needn't show every extreme that they name: `kept_index`: in each window all 64 entries are distinct offsets; the first kept_count of them are the kept tokens in rising order. `kept_count`: every device holds, in its sample, a window with exactly 64 kept tokens.
All inputs are finite; a program needn't handle non-finite values.
Results may differ from a plain program's by a relative error of at most 0.023.
Values may be sent and summed in bfloat16 or wider, within the bound.
A program may use at most 128 MiB of HBM per device.

v0:
```python
import jax
import jax.numpy as jnp
from jax import lax
from jax.sharding import PartitionSpec as P

HEADS = 8
HD = 160


norm_eps = 1e-05
mask_floor = -1e30


def layer_norm(values):
    centre = values - jnp.mean(values, axis=-1, keepdims=True)
    spread = jnp.mean(centre * centre, axis=-1, keepdims=True)
    return centre * lax.rsqrt(spread + norm_eps)


def fold_product(left_rows, shard_rows):
    return jnp.dot(left_rows, shard_rows, preferred_element_type=jnp.float32)


def attend(query_rows, key_rows, value_rows, keep_mask):
    scores = jnp.einsum(
        "bnhd,bmhd->bhnm", query_rows, key_rows, preferred_element_type=jnp.float32
    ) * HD ** (-0.5)
    scores = jnp.where(keep_mask[:, None, None, :], scores, mask_floor)
    scores = scores - jnp.max(scores, axis=-1, keepdims=True)
    weights = jnp.exp(scores)
    probabilities = (weights / jnp.sum(weights, axis=-1, keepdims=True)).astype(jnp.bfloat16)
    blended = jnp.einsum(
        "bhnm,bmhd->bnhd", probabilities, value_rows, preferred_element_type=jnp.float32
    )
    return blended.astype(jnp.bfloat16).reshape(
        query_rows.shape[0], query_rows.shape[1], HEADS * HD
    )


def owner_work(received, flag_rows):
    item_count = received.shape[0]
    slot_values = received.reshape(item_count, -1, received.shape[-1])
    heads_split = slot_values.reshape(item_count, slot_values.shape[1], 3, HEADS, HD)
    keep_mask = flag_rows.reshape(item_count, -1) > 0
    return attend(heads_split[:, :, 0], heads_split[:, :, 1], heads_split[:, :, 2], keep_mask)


def body(patches, kept_index, kept_count, embed_weight, local_qkv, local_out, global_qkv):
    lat_windows = patches.shape[1]
    lon_windows = patches.shape[2]
    windows = lat_windows * lon_windows
    window_tokens = patches.shape[3]
    kept_most = kept_index.shape[3]
    row_count = windows * kept_most
    inner_width = HEADS * HD
    patch_rows = patches.reshape(windows, window_tokens, patches.shape[4])
    index_rows = kept_index.reshape(windows, kept_most)
    kept_mask = lax.broadcasted_iota(jnp.int32, (windows, kept_most), 1) < kept_count.reshape(
        windows, 1
    )
    picked = jnp.take_along_axis(patch_rows, index_rows[:, :, None], axis=1).reshape(row_count, -1)
    embedded = fold_product(
        picked, lax.all_gather(embed_weight, "batch", axis=0, tiled=True)
    ).astype(jnp.bfloat16)
    normed = layer_norm(embedded.astype(jnp.float32)).astype(jnp.bfloat16)
    local_proj = fold_product(
        normed, lax.all_gather(local_qkv, "batch", axis=0, tiled=True)
    ).astype(jnp.bfloat16)
    local_split = local_proj.reshape(windows, kept_most, 3, HEADS, HD)
    local_mix = attend(
        local_split[:, :, 0], local_split[:, :, 1], local_split[:, :, 2], kept_mask
    ).reshape(row_count, inner_width)
    back_sum = fold_product(local_mix, lax.all_gather(local_out, "batch", axis=0, tiled=True))
    hidden = (embedded.astype(jnp.float32) + back_sum).astype(jnp.bfloat16)
    normed_global = layer_norm(hidden.astype(jnp.float32)).astype(jnp.bfloat16)
    outgoing = fold_product(
        normed_global, lax.all_gather(global_qkv, "batch", axis=0, tiled=True)
    ).astype(jnp.bfloat16)
    sent_width = outgoing.shape[1]
    window_ids = lax.broadcasted_iota(jnp.int32, (windows, kept_most), 0)
    slot_rows = (
        jnp.zeros((window_tokens, windows, sent_width), jnp.bfloat16)
        .at[index_rows, window_ids]
        .set(outgoing.reshape(windows, kept_most, sent_width))
    )
    flag_slots = (
        jnp.zeros((window_tokens, windows), jnp.bfloat16)
        .at[index_rows, window_ids]
        .set(kept_mask.astype(jnp.bfloat16))
    )
    lat_size = lax.axis_size("lat")
    lon_size = lax.axis_size("lon")
    owners = lat_size * lon_size
    owned_count = window_tokens // owners
    blended = owner_work(
        lax.all_to_all(
            slot_rows.reshape(owned_count, owners, windows, sent_width),
            ("lat", "lon"),
            split_axis=1,
            concat_axis=2,
            tiled=True,
        ),
        lax.all_to_all(
            flag_slots.reshape(owned_count, owners, windows),
            ("lat", "lon"),
            split_axis=1,
            concat_axis=2,
            tiled=True,
        ),
    )
    shaped = blended.reshape(blended.shape[0], 1, -1, inner_width)
    returned = lax.all_to_all(shaped, ("lat", "lon"), split_axis=2, concat_axis=1, tiled=True)
    out_slots = returned.reshape(window_tokens, windows, inner_width)
    gathered = out_slots[index_rows, window_ids]
    result = jnp.where(kept_mask[:, :, None], gathered, jnp.zeros_like(gathered))
    return result.reshape(1, lat_windows, lon_windows, kept_most, inner_width)


def solution(mesh):
    return jax.shard_map(
        body,
        mesh=mesh,
        in_specs=(
            P("batch", "lat", "lon", None, None),
            P("batch", "lat", "lon", None),
            P("batch", "lat", "lon"),
            P("batch", None),
            P("batch", None),
            P("batch", None),
            P("batch", None),
        ),
        out_specs=P("batch", "lat", "lon", None, None),
        check_vma=False,
    )
```

profile of v0, /device:TPU:1, one launch (start us, length us, event | category | flops | bytes accessed | tf_op | source)
XLA Modules:
  0.0 682.9 jit_solution(14793316787551254619)
XLA Ops:
  6.5 0.7 all-gather.5.cloned.1.call-update
  7.3 0.0 all-gather.7.cloned.1.call-start
  7.3 0.7 all-gather.7.cloned.1.call-update
  8.0 0.0 all-gather.9.cloned.1.call-start
  8.1 0.7 all-gather.9.cloned.1.call-update
  8.8 0.0 all-gather.11.cloned.1.call-start
  8.8 0.5 all-gather.11.cloned.1.call-update
  9.4 0.1 lt.54
  9.5 0.1 reshape.204
  9.6 0.1 fusion.43
  9.6 0.1 reshape.212
  9.7 18.4 %scatter_fusion.1 = bf16[128,6]{0,1:T(8,128)(2,1)S(1)} fusion(bf16[128,6]{0,1:T(8,128)(2,1)S(1)} %broadcast_in_dim.72, s32[384]{0:T(512)S(1)} %reshape.204, bf16[384]{0:T(512)(128)(2,1)S(1)} %reshape.212), kind=kCustom, calls=%fused_computation.3 | custom fusion | bytes 5376 | tf_op jit(solution)/shard_map/scatter | solution.py:89
  28.1 0.1 reshape.190
  28.2 0.7 copy.55
  28.9 13.0 %all-to-all-start.1 = ((bf16[2,64,6]{2,0,1:T(2,128)(2,1)}), bf16[2,64,6]{2,0,1:T(2,128)(2,1)S(1)}, u32[]{:S(2)}, u32[]{:S(2)}) async-start(bf16[2,64,6]{2,0,1:T(2,128)(2,1)} %copy.55), calls=%async_computation.1 | async-start | bytes 65536 | tf_op jit(solution)/shard_map/all_to_all | solution.py:103
  41.9 0.1 reshape.198
  42.0 0.1 broadcast_in_dim_reshape.3
  42.1 4.3 gather_fusion.1
  46.4 0.0 all-gather.5.cloned.1.call-done
  46.5 2.5 convert_reduce_fusion
  49.0 0.4 fusion.11
  49.4 92.6 %all-gather.7.cloned.1.call-done = bf16[1280,3840]{1,0:T(8,128)(2,1)} async-done(((bf16[320,3840]{1,0:T(8,128)(2,1)}), bf16[1280,3840]{1,0:T(8,128)(2,1)}) %all-gather.7.cloned.1.call-update) | async-done | bytes 9830416 | tf_op jit(solution)/shard_map/all_gather | solution.py:67
  142.0 9.4 %convolution_convert_fusion.1 = bf16[384,3840]{1,0:T(8,128)(2,1)} fusion(bf16[1280,3840]{1,0:T(8,128)(2,1)} %all-gather.7.cloned.1.call-done, bf16[384,1280]{1,0:T(8,128)(2,1)S(1)} %get-tuple-element.17, f32[384]{0:T(512)S(1)} %add_rsqrt_fusion.1, f32[384]{0:T(512)S(1)} %broadcast_multiply_fusion.1), kind=kOutput, calls=%fused_computation.11 | convolution fusion | flops 3778314240 | bytes 13765632 | tf_op jit(solution)/shard_map/dot_general | solution.py:21
  151.3 9.2 %reshape.187 = bf16[6,64,3,8,160]{4,3,2,1,0:T(8,128)(2,1)} reshape(bf16[384,3840]{1,0:T(8,128)(2,1)} %convolution_convert_fusion.1) | data formatting | bytes 5898240 | tf_op jit(solution)/shard_map/reshape | solution.py:69
  160.5 2.7 fusion.46
  163.2 0.8 multiply_select_fusion.4
  164.0 1.1 copy-done.5
  165.1 0.4 fusion.47
  165.5 4.0 fusion.22
  169.5 2.3 copy.52
  171.9 2.6 reshape_reshape.9
  174.4 13.5 %all-gather.9.cloned.1.call-done = bf16[1280,1280]{1,0:T(8,128)(2,1)} async-done(((bf16[320,1280]{1,0:T(8,128)(2,1)}), bf16[1280,1280]{1,0:T(8,128)(2,1)}) %all-gather.9.cloned.1.call-update) | async-done | bytes 3276816 | tf_op jit(solution)/shard_map/all_gather | solution.py:73
  188.0 3.8 fusion.48
  191.7 0.3 multiply_reduce_fusion
  192.1 95.6 %all-gather.11.cloned.1.call-done = bf16[1280,3840]{1,0:T(8,128)(2,1)} async-done(((bf16[320,3840]{1,0:T(8,128)(2,1)}), bf16[1280,3840]{1,0:T(8,128)(2,1)}) %all-gather.11.cloned.1.call-update) | async-done | bytes 9830416 | tf_op jit(solution)/shard_map/all_gather | solution.py:77
  287.7 9.2 %convolution_convert_fusion = bf16[384,3840]{1,0:T(8,128)(2,1)} fusion(bf16[1280,3840]{1,0:T(8,128)(2,1)} %all-gather.11.cloned.1.call-done, f32[384,1280]{1,0:T(8,128)S(1)} %get-tuple-element.19, f32[384]{0:T(512)S(1)} %add_rsqrt_fusion, f32[384]{0:T(512)S(1)} %broadcast_multiply_fusion), kind=kOutput, calls=%fused_computation.10 | convolution fusion | flops 3777822720 | bytes 14748672 | tf_op jit(solution)/shard_map/dot_general | solution.py:21
  296.9 3.0 broadcast_in_dim.67
  299.9 96.4 %scatter_fusion = bf16[128,6,3840]{2,0,1:T(8,128)(2,1)} fusion(bf16[128,6,3840]{2,0,1:T(8,128)(2,1)} %broadcast_in_dim.67, s32[384]{0:T(512)S(1)} %reshape.204, bf16[384,3840]{1,0:T(8,128)(2,1)} %convolution_convert_fusion), kind=kCustom, calls=%fused_computation.2 | custom fusion | bytes 8850432 | tf_op jit(solution)/shard_map/scatter | solution.py:84
  396.3 9.8 %copy.53 = bf16[2,64,6,3840]{3,0,2,1:T(2,128)(2,1)} copy(bf16[2,64,6,3840]{3,1,0,2:T(8,128)(2,1)} %bitcast.61) | data formatting | bytes 11796480 | tf_op jit(solution)/shard_map/reshape | solution.py:97
  406.1 0.0 all-to-all-done.1
  406.1 11.8 %all-to-all-start = ((bf16[2,64,6,3840]{3,0,2,1:T(2,128)(2,1)}), bf16[2,64,6,3840]{3,0,2,1:T(2,128)(2,1)}, u32[]{:S(2)}, u32[]{:S(2)}) async-start(bf16[2,64,6,3840]{3,0,2,1:T(2,128)(2,1)} %copy.53), calls=%async_computation | async-start | bytes 11796480 | tf_op jit(solution)/shard_map/all_to_all | solution.py:96
  417.8 0.1 copy.56
  417.9 0.1 copy.57
  418.1 0.2 gt.15
  418.2 132.0 %all-to-all-done = bf16[2,64,6,3840]{3,0,2,1:T(2,128)(2,1)} async-done(((bf16[2,64,6,3840]{3,0,2,1:T(2,128)(2,1)}), bf16[2,64,6,3840]{3,0,2,1:T(2,128)(2,1)}, u32[]{:S(2)}, u32[]{:S(2)}) %all-to-all-start) | async-done | bytes 5898272 | tf_op jit(solution)/shard_map/all_to_all | solution.py:96
  550.3 19.2 %reshape_reshape.10 = bf16[2,384,3,8,160]{4,3,2,0,1:T(8,128)(2,1)} reshape(bf16[2,64,6,3840]{3,0,2,1:T(2,128)(2,1)} %all-to-all-done) | data formatting | bytes 11796480 | tf_op jit(solution)/shard_map/reshape;reshape | solution.py:43
  569.5 7.0 %fusion.45 = (bf16[2,384,1,8,160]{4,3,2,0,1:T(8,128)(2,1)}, bf16[2,384,1,8,160]{4,3,2,0,1:T(8,128)(2,1)}, bf16[2,384,1,8,160]{4,3,2,0,1:T(8,128)(2,1)}) fusion(bf16[2,384,3,8,160]{4,3,2,0,1:T(8,128)(2,1)} %reshape_reshape.10), kind=kLoop, calls=%fused_computation.76 | loop fusion | bytes 11796480 | tf_op jit(solution)/shard_map/slice | solution.py:45
  576.5 3.8 copy.70
  580.3 4.7 copy.71
  585.0 4.8 copy.69
  589.8 3.5 fusion.13
  593.3 4.1 fusion.49
  597.4 1.5 fusion.17
  598.9 4.7 copy.61
  603.6 6.4 all-to-all-start.2
  610.0 0.1 reshape.192
  610.1 0.1 iota_compare_fusion.1
  610.1 48.8 %all-to-all-done.2 = bf16[2,1,384,1280]{3,0,1,2:T(2,128)(2,1)S(1)} async-done(((bf16[2,1,384,1280]{3,0,1,2:T(2,128)(2,1)}), bf16[2,1,384,1280]{3,0,1,2:T(2,128)(2,1)S(1)}, u32[]{:S(2)}, u32[]{:S(2)}) %all-to-all-start.2) | async-done | bytes 1966112 | tf_op jit(solution)/shard_map/all_to_all | solution.py:112
  658.9 1.4 copy.62
  660.4 4.1 reshape.191
  664.5 2.1 copy.63
  666.6 0.0 copy-start.1
  666.6 7.5 %gather_fusion = bf16[384,1280]{1,0:T(8,128)(2,1)} fusion(bf16[128,6,1280]{2,0,1:T(8,128)(2,1)S(1)} %copy.63, s32[384]{0:T(512)S(1)} %reshape.192), kind=kCustom, calls=%fused_computation | custom fusion | bytes 1969152 | tf_op jit(solution)/shard_map/gather | solution.py:114
  674.1 2.3 broadcast_select_fusion
  (21 shorter events, 0.1 us)
Async XLA Ops:
  6.5 35.6 %copy-start = (bf16[1,2,3,128,640]{4,3,2,1,0:T(8,128)(2,1)S(1)}, bf16[1,2,3,128,640]{4,3,2,1,0:T(8,128)(2,1)}, u32[]{:S(2)}) copy-start(bf16[1,2,3,128,640]{4,3,2,1,0:T(8,128)(2,1)} %param.7) | copy-start | bytes 2949124
  6.5 39.9 %all-gather.5.cloned.1.call-start = ((), (), s32[]{:S(2)}) async-start(), calls=%async_computation.3 | async-start | bytes 2048000 | tf_op jit(solution)/shard_map/all_gather | solution.py:63
  7.3 134.7 %all-gather.7.cloned.1.call-start = ((), (), s32[]{:S(2)}) async-start(), calls=%async_computation.4 | async-start | bytes 12288000 | tf_op jit(solution)/shard_map/all_gather | solution.py:67
  8.0 1.3 copy-start.3
  8.0 1.3 copy-start.4
  8.0 179.9 %all-gather.9.cloned.1.call-start = ((), (), s32[]{:S(2)}) async-start(), calls=%async_computation.5 | async-start | bytes 4096000 | tf_op jit(solution)/shard_map/all_gather | solution.py:73
  8.8 278.9 %all-gather.11.cloned.1.call-start = ((), (), s32[]{:S(2)}) async-start(), calls=%async_computation.6 | async-start | bytes 12288000 | tf_op jit(solution)/shard_map/all_gather | solution.py:77
  28.9 377.1 %all-to-all-start.1 = ((bf16[2,64,6]{2,0,1:T(2,128)(2,1)}), bf16[2,64,6]{2,0,1:T(2,128)(2,1)S(1)}, u32[]{:S(2)}, u32[]{:S(2)}) async-start(bf16[2,64,6]{2,0,1:T(2,128)(2,1)} %copy.55), calls=%async_computation.1 | async-start | bytes 65536 | tf_op jit(solution)/shard_map/all_to_all | solution.py:103
  164.0 1.1 copy-start.5
  406.1 144.2 %all-to-all-start = ((bf16[2,64,6,3840]{3,0,2,1:T(2,128)(2,1)}), bf16[2,64,6,3840]{3,0,2,1:T(2,128)(2,1)}, u32[]{:S(2)}, u32[]{:S(2)}) async-start(bf16[2,64,6,3840]{3,0,2,1:T(2,128)(2,1)} %copy.53), calls=%async_computation | async-start | bytes 11796480 | tf_op jit(solution)/shard_map/all_to_all | solution.py:96
  593.3 4.1 copy-start.2
  603.6 55.4 %all-to-all-start.2 = ((bf16[2,1,384,1280]{3,0,1,2:T(2,128)(2,1)}), bf16[2,1,384,1280]{3,0,1,2:T(2,128)(2,1)S(1)}, u32[]{:S(2)}, u32[]{:S(2)}) async-start(bf16[2,1,384,1280]{3,0,1,2:T(2,128)(2,1)} %copy.61), calls=%async_computation.2 | async-start | bytes 3932160 | tf_op jit(solution)/shard_map/all_to_all | solution.py:112
  666.6 9.8 %copy-start.1 = (bf16[1,2,3,128,640]{4,3,2,1,0:T(8,128)(2,1)S(1)}, bf16[1,2,3,128,640]{4,3,2,1,0:T(8,128)(2,1)}, u32[]{:S(2)}) copy-start(bf16[1,2,3,128,640]{4,3,2,1,0:T(8,128)(2,1)} %param.7) | copy-start | bytes 2949124
Sparse Core Ops, SparseCore 0:
  9.1 33.1 all-gather.4
  44.2 97.7 all-gather.6
  143.8 44.1 all-gather.8
  189.6 98.0 all-gather.10
where the time goes:
time: 685 us; the launch traced here: 683 us
  waiting for transfers between devices  385 us (56%)
  local copies, waits for them, and re-layouts  211 us (31%)
  matrix products  34.6 us (5%)
  starting transfers between devices  31.2 us (5%)
  between operations  13.3 us (2%)
  other arithmetic  7.76 us (1%)
    all_to_all x1, waiting for transfers between devices, body(): lax.all_to_all(slot_rows.reshape(owned_count, owners, windows, sent_width...  132 us
    scatter x1, local copies, waits for them, and re-layouts, body(): slot_rows = jnp.zeros((window_tokens, windows, sent_width), jnp.bfloat16)...  96.4 us
    all_gather x1, waiting for transfers between devices, body(): lax.all_gather(global_qkv, 'batch', axis=0, tiled=True)  95.6 us
    all_gather x1, waiting for transfers between devices, body(): lax.all_gather(local_qkv, 'batch', axis=0, tiled=True)  92.6 us
    all_to_all x1, waiting for transfers between devices, body(): lax.all_to_all(shaped, ('lat', 'lon'), split_axis=2, concat_axis=1, tiled...  48.8 us
    dot_general x4, matrix products, fold_product(): return jnp.dot(left_rows, shard_rows, preferred_element_type=jnp.float32)  24.9 us
    another operation x1, local copies, waits for them, and re-layouts, owner_work(): slot_values.reshape(item_count, slot_values.shape[1], 3, HEADS, HD)  19.2 us
    scatter x1, local copies, waits for them, and re-layouts, body(): flag_slots = jnp.zeros((window_tokens, windows), jnp.bfloat16).at[index_r...  18.4 us
  transfers between devices with their start and end apart: 7, of which 5 were waited for; matrix products, arithmetic and copies ran while one was open for 27% of the time, Pallas kernels for 0%

commit v1 on v0

v1 whole, which is shorter than its diff:
```python
import jax
import jax.numpy as jnp
from jax import lax
from jax.sharding import PartitionSpec as P

HEADS = 8
HD = 160


norm_eps = 1e-05
mask_floor = -1e30


def layer_norm(values):
    centre = values - jnp.mean(values, axis=-1, keepdims=True)
    spread = jnp.mean(centre * centre, axis=-1, keepdims=True)
    return centre * lax.rsqrt(spread + norm_eps)


def product(left_rows, right_rows):
    return jnp.dot(left_rows, right_rows, preferred_element_type=jnp.float32)


def gather_weight(shard):
    rows = shard.shape[0] // lax.axis_size("lat")
    piece = lax.dynamic_slice_in_dim(shard, lax.axis_index("lat") * rows, rows, 0)
    return lax.all_gather(piece, ("batch", "lat"), axis=0, tiled=True)


def attend(proj, keep_mask):
    groups, rows = proj.shape[:2]
    split = proj.reshape(groups, rows, 3, HEADS, HD)
    scores = jnp.einsum(
        "bnhd,bmhd->bhnm", split[:, :, 0], split[:, :, 1], preferred_element_type=jnp.float32
    ) * HD ** (-0.5)
    scores = jnp.where(keep_mask[:, None, None, :], scores, mask_floor)
    scores = scores - jnp.max(scores, axis=-1, keepdims=True)
    weights = jnp.exp(scores)
    probabilities = (weights / jnp.sum(weights, axis=-1, keepdims=True)).astype(jnp.bfloat16)
    blended = jnp.einsum(
        "bhnm,bmhd->bnhd", probabilities, split[:, :, 2], preferred_element_type=jnp.float32
    )
    return blended.astype(jnp.bfloat16).reshape(groups, rows, HEADS * HD)


def body(patches, kept_index, kept_count, embed_weight, local_qkv, local_out, global_qkv):
    lat_windows = patches.shape[1]
    lon_windows = patches.shape[2]
    windows = lat_windows * lon_windows
    tokens = patches.shape[3]
    most = kept_index.shape[3]
    rows = windows * most
    inner = HEADS * HD
    owners = lax.axis_size("lat") * lax.axis_size("lon")
    owned = tokens // owners
    me = lax.axis_index("lat") * lax.axis_size("lon") + lax.axis_index("lon")

    patch_rows = patches.reshape(windows, tokens, patches.shape[4])
    kept = lax.broadcasted_iota(jnp.int32, (windows, most), 1) < kept_count.reshape(windows, 1)
    marks = jnp.where(kept, kept_index.reshape(windows, most), -1)
    all_marks = lax.all_gather(marks, ("lat", "lon"), axis=0, tiled=True)
    wanted = me + owners * lax.broadcasted_iota(jnp.int32, (owned, 1, 1), 0)
    member = jnp.any(all_marks[None] == wanted, axis=-1)

    chosen = (
        marks[:, :, None] == lax.broadcasted_iota(jnp.int32, (windows, most, tokens), 2)
    ).astype(jnp.bfloat16)
    picked = jnp.einsum(
        "wkt,wtd->wkd", chosen, patch_rows, preferred_element_type=jnp.float32
    ).astype(jnp.bfloat16).reshape(rows, -1)
    embedded = product(picked, gather_weight(embed_weight)).astype(jnp.bfloat16)
    normed = layer_norm(embedded.astype(jnp.float32)).astype(jnp.bfloat16)
    local_proj = product(normed, gather_weight(local_qkv)).astype(jnp.bfloat16)
    local_mix = attend(local_proj.reshape(windows, most, -1), kept).reshape(rows, inner)
    hidden = (
        embedded.astype(jnp.float32) + product(local_mix, gather_weight(local_out))
    ).astype(jnp.bfloat16)
    normed_global = layer_norm(hidden.astype(jnp.float32)).astype(jnp.bfloat16)
    slots = jnp.einsum(
        "wkt,wkd->twd",
        chosen,
        normed_global.reshape(windows, most, -1),
        preferred_element_type=jnp.float32,
    ).astype(jnp.bfloat16)
    received = lax.all_to_all(
        slots.reshape(owned, owners, windows, -1),
        ("lat", "lon"),
        split_axis=1,
        concat_axis=1,
        tiled=True,
    )
    group = owners * windows
    global_proj = product(received.reshape(owned * group, -1), gather_weight(global_qkv))
    blended = attend(
        global_proj.astype(jnp.bfloat16).reshape(owned, group, -1), member.reshape(owned, group)
    )
    returned = lax.all_to_all(
        blended.reshape(owned, owners, windows, inner),
        ("lat", "lon"),
        split_axis=1,
        concat_axis=1,
        tiled=True,
    ).reshape(tokens, windows, inner)
    result = jnp.einsum(
        "wkt,twd->wkd", chosen, returned, preferred_element_type=jnp.float32
    ).astype(jnp.bfloat16)
    return result.reshape(1, lat_windows, lon_windows, most, inner)


def solution(mesh):
    return jax.shard_map(
        body,
        mesh=mesh,
        in_specs=(
            P("batch", "lat", "lon", None, None),
            P("batch", "lat", "lon", None),
            P("batch", "lat", "lon"),
            P("batch", None),
            P("batch", None),
            P("batch", None),
            P("batch", None),
        ),
        out_specs=P("batch", "lat", "lon", None, None),
        check_vma=False,
    )
```

time: 685 us -> 423 us (0.62)
  waiting for transfers between devices: 385 us -> 128 us
  blocking collectives: 0 us -> 140 us
  local copies, waits for them, and re-layouts: 211 us -> 83.2 us
  starting transfers between devices: 31.2 us -> 9.74 us
    all_to_all x3 -> x1, waiting for transfers between devices: 181 us -> 0.01 us  [body(): lax.all_to_all(slots.reshape(owned, owners, windows, -1), ('lat', 'lon'),...]
    scatter x2 -> x0, local copies, waits for them, and re-layouts: 115 us -> none  [the longest x1 96.4 us: body(): slot_rows = jnp.zeros((window_tokens, windows, sent_width), jnp.bfloat16)...]
    all_gather x0 -> x1, blocking collectives: none -> 83.2 us  [body(): all_marks = lax.all_gather(marks, ('lat', 'lon'), axis=0, tiled=True)]
    all_gather x4, waiting for transfers between devices: 202 us -> 128 us  [gather_weight(): return lax.all_gather(piece, ('batch', 'lat'), axis=0, tiled=True)]
    all_to_all x0 -> x1, blocking collectives: none -> 57.1 us  [body(): lax.all_to_all(blended.reshape(owned, owners, windows, inner), ('lat', 'l...]
    all_to_all x3 -> x1, starting transfers between devices: 31.1 us -> 9.58 us  [body(): lax.all_to_all(slots.reshape(owned, owners, windows, -1), ('lat', 'lon'),...]
    reshape x6 -> x3, local copies, waits for them, and re-layouts: 25.9 us -> 6.07 us  [the longest x1 3.3 us: body(): slots.reshape(owned, owners, windows, -1)]
    gather x3 -> x0, local copies, waits for them, and re-layouts: 11.9 us -> none  [the longest x1 7.54 us: body(): gathered = out_slots[index_rows, window_ids]]
  transfers between devices with their start and end apart: 7 -> 5, of which waited for: 5 -> 3; matrix products, arithmetic and copies ran while one was open for 27% -> 13% of each run, Pallas kernels for 0% -> 0%
where the time goes in v1:
time: 423 us; the launch traced here: 422 us
  blocking collectives  140 us (33%)
  waiting for transfers between devices  128 us (30%)
  local copies, waits for them, and re-layouts  83.2 us (20%)
  matrix products  40.9 us (10%)
  between operations  13.3 us (3%)
  starting transfers between devices  9.74 us (2%)
  other arithmetic  5.86 us (1%)
    all_gather x4, waiting for transfers between devices, gather_weight(): return lax.all_gather(piece, ('batch', 'lat'), axis=0, tiled=True)  128 us
    all_gather x1, blocking collectives, body(): all_marks = lax.all_gather(marks, ('lat', 'lon'), axis=0, tiled=True)  83.2 us
    all_to_all x1, blocking collectives, body(): lax.all_to_all(blended.reshape(owned, owners, windows, inner), ('lat', 'l...  57.1 us
    dot_general x4, matrix products, product(): return jnp.dot(left_rows, right_rows, preferred_element_type=jnp.float32)  27.4 us
    another operation x2, local copies, waits for them, and re-layouts, attend(): split = proj.reshape(groups, rows, 3, HEADS, HD)  25.8 us
    unnamed x22, local copies, waits for them, and re-layouts  18.8 us
    all_to_all x1, starting transfers between devices, body(): lax.all_to_all(slots.reshape(owned, owners, windows, -1), ('lat', 'lon'),...  9.58 us
  transfers between devices with their start and end apart: 5, of which 3 were waited for; matrix products, arithmetic and copies ran while one was open for 13% of the time, Pallas kernels for 0%

profile of v1, /device:TPU:1, one launch (start us, length us, event | category | flops | bytes accessed | tf_op | source)
XLA Modules:
  0.0 421.8 jit_solution(6911432130226525416)
XLA Ops:
  6.5 0.0 copy-start
  6.5 0.0 all-gather.13.cloned.1.call-start
  6.6 1.7 dynamic-slice_bitcast_fusion
  8.3 0.0 all-gather.13.cloned.1.call-update
  8.3 0.0 all-gather.7.cloned.1.call-start
  8.4 0.0 copy-done
  8.4 0.7 constant_dynamic-slice_fusion.2
  9.1 0.0 all-gather.7.cloned.1.call-update
  9.1 0.0 all-gather.9.cloned.1.call-start
  9.2 1.5 constant_dynamic-slice_fusion.1
  10.7 0.0 all-gather.9.cloned.1.call-update
  10.8 0.0 all-gather.11.cloned.1.call-start
  10.8 1.7 constant_dynamic-slice_fusion
  12.6 0.0 all-gather.11.cloned.1.call-update
  12.6 0.0 copy-done.5
  12.6 0.1 lt.26
  12.7 0.0 copy-done.4
  12.7 0.1 iota_compare_fusion.4
  12.8 0.1 broadcast_select_fusion
  12.8 0.3 convolution_convert_fusion.6
  13.2 49.4 %all-gather.13.cloned.1.call-done = bf16[32,20,1280]{2,1,0:T(8,128)(2,1)} async-done(((bf16[1,20,1280]{2,1,0:T(8,128)(2,1)}), bf16[32,20,1280]{2,1,0:T(8,128)(2,1)}) %all-gather.13.cloned.1.call-update) | async-done | bytes 1638416 | tf_op jit(solution)/shard_map/all_gather | solution.py:27
  62.6 2.5 reshape.115
  65.1 1.0 convert_reduce_fusion
  66.1 0.4 fusion.11
  66.5 59.2 %all-gather.7.cloned.1.call-done = bf16[1280,3840]{1,0:T(8,128)(2,1)} async-done(((bf16[40,3840]{1,0:T(8,128)(2,1)}), bf16[1280,3840]{1,0:T(8,128)(2,1)}) %all-gather.7.cloned.1.call-update) | async-done | bytes 9830416 | tf_op jit(solution)/shard_map/all_gather | solution.py:27
  125.7 9.4 %convolution_convert_fusion.1 = bf16[384,3840]{1,0:T(8,128)(2,1)} fusion(bf16[1280,3840]{1,0:T(8,128)(2,1)} %all-gather.7.cloned.1.call-done, bf16[384,1280]{1,0:T(8,128)(2,1)S(1)} %get-tuple-element.12, f32[384]{0:T(512)S(1)} %add_rsqrt_fusion.1, f32[384]{0:T(512)S(1)} %broadcast_multiply_fusion.1), kind=kOutput, calls=%fused_computation.7 | convolution fusion | flops 3778314240 | bytes 13765632 | tf_op jit(solution)/shard_map/dot_general | solution.py:21
  135.1 9.2 %reshape_reshape.12 = bf16[6,64,3,8,160]{4,3,2,1,0:T(8,128)(2,1)} reshape(bf16[384,3840]{1,0:T(8,128)(2,1)} %convolution_convert_fusion.1) | data formatting | bytes 5898240 | tf_op jit(solution)/shard_map/reshape;reshape | solution.py:32
  144.2 2.8 fusion.34
  147.0 0.8 multiply_select_fusion.4
  147.8 1.1 copy-done.6
  148.9 0.4 fusion.35
  149.3 4.0 fusion.21
  153.4 2.3 copy.51
  155.7 2.5 reshape_reshape.13
  158.2 19.7 %all-gather.9.cloned.1.call-done = bf16[1280,1280]{1,0:T(8,128)(2,1)} async-done(((bf16[40,1280]{1,0:T(8,128)(2,1)}), bf16[1280,1280]{1,0:T(8,128)(2,1)}) %all-gather.9.cloned.1.call-update) | async-done | bytes 3276816 | tf_op jit(solution)/shard_map/all_gather | solution.py:27
  177.9 3.8 fusion.36
  181.6 0.3 multiply_reduce_fusion
  182.0 0.3 multiply_convert_fusion
  182.3 0.8 convolution_convert_fusion.2
  183.1 3.3 copy.52
  186.4 9.6 %all-to-all-start = ((bf16[2,64,6,1280]{3,0,2,1:T(2,128)(2,1)}), bf16[2,64,6,1280]{3,0,2,1:T(2,128)(2,1)S(1)}, u32[]{:S(2)}, u32[]{:S(2)}) async-start(bf16[2,64,6,1280]{3,0,2,1:T(2,128)(2,1)} %copy.52), calls=%async_computation | async-start | bytes 3932160 | tf_op jit(solution)/shard_map/all_to_all | solution.py:85
  195.9 0.1 fusion.50
  196.0 83.2 %all-gather.1 = s32[64,6,64]{2,1,0:T(8,128)S(1)} all-gather(s32[1,6,64]{2,1,0:T(8,128)S(1)} %fusion.50), channel_id=1, replica_groups=mesh['batch'=4,'lat'=8,'lon'=8] {'lat','lon'}, dimensions={0}, use_global_device_ids=true | all-gather | bytes 99840 | tf_op jit(solution)/shard_map/all_gather | solution.py:61
  279.2 0.1 copy.56
  279.4 0.1 compare_reduce_fusion
  279.5 0.0 all-to-all-done
  279.5 1.8 copy.53
  281.3 2.8 reshape.111
  284.1 0.0 all-gather.11.cloned.1.call-done
  284.1 13.2 %convolution_convert_fusion = bf16[768,3840]{1,0:T(8,128)(2,1)} fusion(bf16[768,1280]{1,0:T(8,128)(2,1)S(1)} %reshape.111, bf16[1280,3840]{1,0:T(8,128)(2,1)} %all-gather.11.cloned.1.call-done), kind=kOutput, calls=%fused_computation.6 | convolution fusion | flops 7552696320 | bytes 17694720 | tf_op jit(solution)/shard_map/dot_general | solution.py:21
  297.3 16.6 %reshape.118 = bf16[2,384,3,8,160]{4,3,2,1,0:T(8,128)(2,1)} reshape(bf16[768,3840]{1,0:T(8,128)(2,1)} %convolution_convert_fusion) | data formatting | bytes 11796480 | tf_op jit(solution)/shard_map/reshape;reshape | solution.py:32
  313.9 7.0 %fusion.33 = (bf16[2,384,1,8,160]{4,3,2,1,0:T(8,128)(2,1)}, bf16[2,384,1,8,160]{4,3,2,1,0:T(8,128)(2,1)}, bf16[2,384,1,8,160]{4,3,2,1,0:T(8,128)(2,1)}) fusion(bf16[2,384,3,8,160]{4,3,2,1,0:T(8,128)(2,1)} %reshape.118), kind=kLoop, calls=%fused_computation.64 | loop fusion | bytes 11796480 | tf_op jit(solution)/shard_map/slice | solution.py:41
  320.9 3.8 copy.70
  324.7 4.7 %copy.71 = bf16[2,384,1,8,160]{1,4,3,0,2:T(8,128)(2,1)} copy(bf16[2,384,1,8,160]{4,3,2,1,0:T(8,128)(2,1)} %get-tuple-element.7) | data formatting | bytes 3932160
  329.4 4.8 %copy.69 = bf16[2,384,1,8,160]{1,4,3,0,2:T(8,128)(2,1)} copy(bf16[2,384,1,8,160]{4,3,2,1,0:T(8,128)(2,1)} %get-tuple-element.5) | data formatting | bytes 3932160
  334.2 3.5 fusion.13
  337.7 4.1 fusion.37
  341.8 2.8 convert_bitcast_fusion
  344.6 5.0 %copy.60 = bf16[2,384,8,160]{3,2,0,1:T(8,128)(2,1)} copy(bf16[2,384,8,160]{1,3,2,0:T(8,128)(2,1)} %convert_bitcast_fusion) | data formatting | bytes 3932160 | tf_op jit(solution)/shard_map/convert_element_type | solution.py:43
  349.6 6.9 %reshape_reshape.15 = bf16[2,64,6,1280]{3,0,2,1:T(2,128)(2,1)S(1)} reshape(bf16[2,384,8,160]{3,2,0,1:T(8,128)(2,1)} %copy.60) | data formatting | bytes 3932160 | tf_op jit(solution)/shard_map/reshape;reshape | solution.py:98
  356.4 57.1 %all_to_all.10 = bf16[2,64,6,1280]{3,0,2,1:T(2,128)(2,1)S(1)} all-to-all(bf16[2,64,6,1280]{3,0,2,1:T(2,128)(2,1)S(1)} %reshape_reshape.15), channel_id=1, replica_groups=mesh['batch'=4,'lat'=8,'lon'=8] {'lat','lon'}, dimensions={1} | all-to-all | bytes 3932160 | tf_op jit(solution)/shard_map/all_to_all | solution.py:97
  413.6 0.2 copy.61
  413.8 1.4 convolution_convert_fusion.3
  415.2 0.0 copy-done.1
  (16 shorter events, 0.1 us)
Async XLA Ops:
  6.5 1.8 copy-start
  6.5 6.0 %copy-start.5 = (s32[1,2,3]{2,1,0:T(2,128)S(1)}, s32[1,2,3]{2,1,0:T(2,128)}, u32[]{:S(2)}) copy-start(s32[1,2,3]{2,1,0:T(2,128)} %param.9) | copy-start | bytes 76
  6.5 6.1 %copy-start.4 = (s32[1,2,3,64]{3,1,2,0:T(2,128)S(1)}, s32[1,2,3,64]{3,1,2,0:T(2,128)}, u32[]{:S(2)}) copy-start(s32[1,2,3,64]{3,1,2,0:T(2,128)} %param.8) | copy-start | bytes 4612
  6.5 6.3 %copy-start.3 = (bf16[1,2,3,128,640]{4,3,2,1,0:T(8,128)(2,1)S(1)}, bf16[1,2,3,128,640]{4,3,2,1,0:T(8,128)(2,1)}, u32[]{:S(2)}) copy-start(bf16[1,2,3,128,640]{4,3,2,1,0:T(8,128)(2,1)} %param.7) | copy-start | bytes 2949124
  6.5 56.1 %all-gather.13.cloned.1.call-start = ((), (), s32[]{:S(2)}) async-start(), calls=%async_computation.5 | async-start | bytes 2027520 | tf_op jit(solution)/shard_map/all_gather | solution.py:27
  8.3 117.4 %all-gather.7.cloned.1.call-start = ((), (), s32[]{:S(2)}) async-start(), calls=%async_computation.2 | async-start | bytes 10137600 | tf_op jit(solution)/shard_map/all_gather | solution.py:27
  9.1 168.7 %all-gather.9.cloned.1.call-start = ((), (), s32[]{:S(2)}) async-start(), calls=%async_computation.3 | async-start | bytes 3379200 | tf_op jit(solution)/shard_map/all_gather | solution.py:27
  10.8 273.3 %all-gather.11.cloned.1.call-start = ((), (), s32[]{:S(2)}) async-start(), calls=%async_computation.4 | async-start | bytes 10137600 | tf_op jit(solution)/shard_map/all_gather | solution.py:27
  147.8 1.1 copy-start.6
  186.4 93.1 %all-to-all-start = ((bf16[2,64,6,1280]{3,0,2,1:T(2,128)(2,1)}), bf16[2,64,6,1280]{3,0,2,1:T(2,128)(2,1)S(1)}, u32[]{:S(2)}, u32[]{:S(2)}) async-start(bf16[2,64,6,1280]{3,0,2,1:T(2,128)(2,1)} %copy.52), calls=%async_computation | async-start | bytes 3932160 | tf_op jit(solution)/shard_map/all_to_all | solution.py:85
  337.7 4.1 copy-start.2
  413.6 1.7 copy-start.1
Sparse Core Ops, SparseCore 0:
  10.0 52.6 all-gather.12
  65.2 60.4 all-gather.6
  128.3 49.5 all-gather.8
  180.4 74.4 all-gather.10
